TPU v7x, 32 devices: a whole 2x2x4 slice. The times are simulated.
32 devices in a mesh: dp: 4 (over x, core), expert: 8 (over z, y).
Axes of the slice: x: 2, y: 2, z: 4, core: 2. Of those that a mesh axis runs over, the one named last changes fastest.
Arguments:
- hidden_in: bfloat16 [8192, 1024], P(('dp', 'expert')), may hold values from -6 to 6
- d_out: bfloat16 [8192, 1024], P(('dp', 'expert')), may hold values from -6 to 6
- gain_attn: bfloat16 [1024], P('dp'), may hold values from 0.25 to 1.75
- w_qkv: bfloat16 [1024, 2048], P('dp'), may hold values from -0.1875 to 0.1875
- w_o: bfloat16 [1024, 1024], P('dp'), may hold values from -1.5 to 1.5
- gain_moe: bfloat16 [1024], P('dp'), may hold values from 0.25 to 1.75
- w_router: bfloat16 [1024, 16], P('dp'), may hold values from -0.375 to 0.375
- w_in: bfloat16 [16, 1024, 1024], P('expert', 'dp'), may hold values from -0.1875 to 0.1875
- w_out: bfloat16 [16, 512, 1024], P('expert', None, 'dp'), may hold values from -0.75 to 0.75
- seq_lengths: int32 [4, 4], P('dp'), may hold values from 1 to 1024, 2048 in all within a row
- assign: int32 [4, 2048], P('dp', 'expert'), may hold values from 0 to 2047, each once within a row
- routes: int32 [8192, 8], P(('dp', 'expert')), may hold values from 0 to 15, all different within a row; in each aligned block of 256 rows (0 to 255, 256 to 511, ...) at most 192 rows name the same one
Outputs:
- layer_out: bfloat16 [8192, 1024], P(('dp', 'expert'))
- grad_in: float32 [8192, 1024], P(('dp', 'expert'))
- grad_gain_attn: float32 [1024], P('dp')
- grad_w_qkv: float32 [1024, 2048], P('dp')
- grad_w_o: float32 [1024, 1024], P('dp')
- grad_gain_moe: float32 [1024], P('dp')
- grad_w_router: float32 [1024, 16], P('dp')
- grad_w_in: float32 [16, 1024, 1024], P('expert', 'dp')
- grad_w_out: float32 [16, 512, 1024], P('expert', None, 'dp')
Inputs may be any that keep to these rules, and one draw needn't show every extreme that they name: `assign`: each row of a batch group's stream positions names every position of the group once. `seq_lengths`: each row holds 4 lengths that sum to 2048; the longest is 1024. `routes`: A token names 8 different experts. Within the rows of one device no expert is named by more than 192 rows, and in every draw some device has an expert named by exactly 192 of its rows.
All inputs are finite; a program needn't handle non-finite values.
Results may differ from a plain program's by a relative error of at most 0.015.
Values may be sent and summed in bfloat16 or wider, within the bound.
A program may use at most 192 MiB of HBM per device.

v0:
```python
import jax
import jax.numpy as jnp
from jax import lax
from jax.sharding import PartitionSpec as P

D = 1024
HEADS = 16
KV_HEADS = 8
HEAD_DIM = 64


EPSILON = 1e-06
ROPE_BASE = 10000.0
SCORE_SCALE = 0.015625
MASKED = -1e30


def rms_norm(values, gain_vec):
    factor = lax.rsqrt(jnp.mean(values * values, axis=-1, keepdims=True) + EPSILON)
    return values * factor * gain_vec


def rotary_tables(positions):
    half_dim = HEAD_DIM // 2
    exponent = jnp.arange(half_dim).astype(jnp.float32) * (2.0 / HEAD_DIM)
    frequency = ROPE_BASE ** (-exponent)
    angles = positions.astype(jnp.float32)[:, None] * frequency[None, :]
    angles = jnp.concatenate([angles, angles], axis=1)
    return (jnp.cos(angles), jnp.sin(angles))


def rotate(values, cosine_tab, sine_tab):
    half_dim = HEAD_DIM // 2
    turned = jnp.concatenate([-values[..., half_dim:], values[..., :half_dim]], axis=-1)
    return values * cosine_tab[:, None, :] + turned * sine_tab[:, None, :]


def rotate_back(grads, cosine_tab, sine_tab):
    half_dim = HEAD_DIM // 2
    scaled = grads * sine_tab[:, None, :]
    turned = jnp.concatenate([scaled[..., half_dim:], -scaled[..., :half_dim]], axis=-1)
    return grads * cosine_tab[:, None, :] + turned


def stream_info(assigned, seq_lengths):
    seq_ends = jnp.cumsum(seq_lengths)
    seq_starts = seq_ends - seq_lengths
    seq_id = jnp.sum((assigned[:, None] >= seq_ends[None, :]).astype(jnp.int32), axis=1)
    matches = seq_id[:, None] == jnp.arange(seq_lengths.shape[0], dtype=jnp.int32)[None, :]
    start_of = jnp.sum(jnp.where(matches, seq_starts[None, :], 0), axis=1)
    return (seq_id, assigned - start_of)


def gate_up_grad(gate_pre, up_pre, d_hidden):
    sigmoid = jax.nn.sigmoid(gate_pre)
    activated = gate_pre * sigmoid
    d_gate = d_hidden * up_pre * sigmoid * (1.0 + gate_pre * (1.0 - sigmoid))
    return jnp.concatenate([d_gate, d_hidden * activated], axis=-1)


def expert_front(rows_in, weight_in, weight_out):
    gate_up = jnp.einsum("sltd,ldf->sltf", rows_in, weight_in, preferred_element_type=jnp.float32)
    half_width = gate_up.shape[-1] // 2
    hidden = (jax.nn.silu(gate_up[..., :half_width]) * gate_up[..., half_width:]).astype(
        jnp.bfloat16
    )
    produced = jnp.einsum(
        "sltf,lfd->sltd", hidden, weight_out, preferred_element_type=jnp.float32
    ).astype(jnp.bfloat16)
    return (gate_up, hidden, produced)


def expert_rear(gate_up, d_arrived, weight_in, weight_out):
    half_width = gate_up.shape[-1] // 2
    d_hidden = jnp.einsum(
        "sltd,lfd->sltf", d_arrived, weight_out, preferred_element_type=jnp.float32
    )
    d_gate_up = gate_up_grad(gate_up[..., :half_width], gate_up[..., half_width:], d_hidden).astype(
        jnp.bfloat16
    )
    d_slots = jnp.einsum(
        "sltf,ldf->sltd", d_gate_up, weight_in, preferred_element_type=jnp.float32
    ).astype(jnp.bfloat16)
    return (d_gate_up, d_slots)


def block_scores(query_grp, key_blk, query_pos, query_seg, key_pos, key_seg):
    scores = (
        jnp.einsum("tgrd,kgd->tgrk", query_grp, key_blk, preferred_element_type=jnp.float32)
        * SCORE_SCALE
    )
    allowed = (query_seg[:, None] == key_seg[None, :]) & (key_pos[None, :] <= query_pos[:, None])
    return jnp.where(allowed[:, None, None, :], scores, MASKED)


def local(
    hidden_in,
    d_out,
    gain_attn,
    w_qkv,
    w_o,
    gain_moe,
    w_router,
    w_in,
    w_out,
    seq_lengths,
    assign,
    routes,
):
    tok_rows = hidden_in.shape[0]
    top_count = routes.shape[1]
    exp_dev = w_in.shape[0]
    n_expert = lax.axis_size("expert")
    experts = exp_dev * n_expert
    capacity = 3 * tok_rows * top_count // (2 * experts)
    groups = HEADS // KV_HEADS
    q_cols = HEADS * HEAD_DIM
    k_cols = KV_HEADS * HEAD_DIM
    gain_full, qkv_full, proj_full, gain_full_two, router_full = (
        lax.all_gather(gain_attn, "dp", axis=0, tiled=True),
        lax.all_gather(w_qkv, "dp", axis=0, tiled=True),
        lax.all_gather(w_o, "dp", axis=0, tiled=True),
        lax.all_gather(gain_moe, "dp", axis=0, tiled=True),
        lax.all_gather(w_router, "dp", axis=0, tiled=True),
    )
    gain_one = gain_full.astype(jnp.float32)
    gain_two = gain_full_two.astype(jnp.float32)
    weight_in, weight_out = (
        lax.all_gather(w_in, "dp", axis=1, tiled=True),
        lax.all_gather(w_out, "dp", axis=2, tiled=True),
    )
    positions = assign[0]
    segments, rot_pos = stream_info(positions, seq_lengths[0])
    cosine_tab, sine_tab = rotary_tables(rot_pos)
    stream_in = hidden_in.astype(jnp.float32)
    normed_one = rms_norm(stream_in, gain_one).astype(jnp.bfloat16)
    projected = jnp.dot(normed_one, qkv_full, preferred_element_type=jnp.float32)
    query_rot = rotate(
        projected[:, :q_cols].reshape(tok_rows, HEADS, HEAD_DIM), cosine_tab, sine_tab
    ).astype(jnp.bfloat16)
    key_rot = rotate(
        projected[:, q_cols : q_cols + k_cols].reshape(tok_rows, KV_HEADS, HEAD_DIM),
        cosine_tab,
        sine_tab,
    ).astype(jnp.bfloat16)
    kv_local = jnp.concatenate(
        [key_rot.reshape(tok_rows, k_cols), projected[:, q_cols + k_cols :].astype(jnp.bfloat16)],
        axis=1,
    )
    key_all, pos_all, seg_all = (
        lax.all_gather(kv_local, "expert", axis=0, tiled=True),
        lax.all_gather(positions, "expert", axis=0, tiled=True),
        lax.all_gather(segments, "expert", axis=0, tiled=True),
    )
    group_rows = key_all.shape[0]
    key_block = min(512, group_rows)
    block_count = group_rows // key_block
    query_grp = query_rot.reshape(tok_rows, KV_HEADS, groups, HEAD_DIM)
    key_blocks = key_all[:, :k_cols].reshape(block_count, key_block, KV_HEADS, HEAD_DIM)
    value_blocks = key_all[:, k_cols:].reshape(block_count, key_block, KV_HEADS, HEAD_DIM)
    pos_blocks = pos_all.reshape(block_count, key_block)
    seg_blocks = seg_all.reshape(block_count, key_block)

    def max_step(running, inputs):
        run_max, run_total = running
        key_blk, key_pos, key_seg = inputs
        scores = block_scores(query_grp, key_blk, positions, segments, key_pos, key_seg)
        new_max = jnp.maximum(run_max, jnp.max(scores, axis=-1))
        run_total = run_total * jnp.exp(run_max - new_max) + jnp.sum(
            jnp.exp(scores - new_max[..., None]), axis=-1
        )
        return ((new_max, run_total), None)

    start_max = jnp.full((tok_rows, KV_HEADS, groups), MASKED, jnp.float32)
    start_total = jnp.zeros((tok_rows, KV_HEADS, groups), jnp.float32)
    (run_max, run_total), unused = lax.scan(
        max_step, (start_max, start_total), (key_blocks, pos_blocks, seg_blocks)
    )
    log_total = run_max + jnp.log(run_total)

    def value_step(running, inputs):
        key_blk, value_blk, key_pos, key_seg = inputs
        scores = block_scores(query_grp, key_blk, positions, segments, key_pos, key_seg)
        soft_weights = jnp.exp(scores - log_total[..., None]).astype(jnp.bfloat16)
        return (
            running
            + jnp.einsum(
                "tgrk,kgd->tgrd", soft_weights, value_blk, preferred_element_type=jnp.float32
            ),
            None,
        )

    start_out = jnp.zeros((tok_rows, KV_HEADS, groups, HEAD_DIM), jnp.float32)
    attended_sum, unused = lax.scan(
        value_step, start_out, (key_blocks, value_blocks, pos_blocks, seg_blocks)
    )
    attended = attended_sum.astype(jnp.bfloat16)
    attended_flat = attended.reshape(tok_rows, q_cols)
    mid_stream = stream_in + jnp.dot(attended_flat, proj_full, preferred_element_type=jnp.float32)
    normed_two = rms_norm(mid_stream, gain_two).astype(jnp.bfloat16)
    logits = jnp.dot(normed_two, router_full, preferred_element_type=jnp.float32)
    gate_probs = jax.nn.softmax(jnp.take_along_axis(logits, routes, axis=1), axis=1)
    expert_ids = jnp.arange(experts, dtype=jnp.int32)
    route_hits = (routes[:, :, None] == expert_ids[None, None, :]).astype(jnp.int32)
    per_row = jnp.sum(route_hits, axis=1)
    before = jnp.cumsum(per_row, axis=0) - per_row
    slot_of = jnp.sum(route_hits * before[:, None, :], axis=2)
    target = (routes * capacity + slot_of).reshape(-1)
    outgoing = (
        jnp.zeros((experts * capacity, D), jnp.bfloat16)
        .at[target]
        .set(jnp.repeat(normed_two, top_count, axis=0))
    )
    outgoing = outgoing.reshape(n_expert, exp_dev, capacity, D)
    cotangent = d_out.astype(jnp.float32)
    d_sent = (
        (gate_probs[:, :, None] * cotangent[:, None, :])
        .astype(jnp.bfloat16)
        .reshape(tok_rows * top_count, D)
    )
    d_outgoing = jnp.zeros((experts * capacity, D), jnp.bfloat16).at[target].set(d_sent)
    d_outgoing = d_outgoing.reshape(n_expert, exp_dev, capacity, D)
    received_rows = lax.all_to_all(outgoing, "expert", split_axis=0, concat_axis=0, tiled=True)
    gate_up, hidden_rows, produced = expert_front(received_rows, weight_in, weight_out)
    returned_rows = lax.all_to_all(produced, "expert", split_axis=0, concat_axis=0, tiled=True)
    d_received = lax.all_to_all(d_outgoing, "expert", split_axis=0, concat_axis=0, tiled=True)
    d_gate_up, d_slots = expert_rear(gate_up, d_received, weight_in, weight_out)
    d_returned = lax.all_to_all(d_slots, "expert", split_axis=0, concat_axis=0, tiled=True)
    back_rows = returned_rows.reshape(experts * capacity, D)[target].reshape(tok_rows, top_count, D)
    back_wide = back_rows.astype(jnp.float32)
    moe_sum = jnp.einsum("tj,tjd->td", gate_probs, back_wide)
    layer_out = (mid_stream + moe_sum).astype(jnp.bfloat16)
    d_gate = jnp.einsum("td,tjd->tj", cotangent, back_wide)
    grad_out_local = jnp.einsum(
        "sltf,sltd->lfd", hidden_rows, d_received, preferred_element_type=jnp.float32
    )
    grad_in_local = jnp.einsum(
        "sltd,sltf->ldf", received_rows, d_gate_up, preferred_element_type=jnp.float32
    )
    grad_w_in, grad_w_out = (
        lax.psum_scatter(grad_in_local, "dp", scatter_dimension=1, tiled=True),
        lax.psum_scatter(grad_out_local, "dp", scatter_dimension=2, tiled=True),
    )
    d_rows = d_returned.reshape(experts * capacity, D)[target].reshape(tok_rows, top_count, D)
    d_chosen = gate_probs * (d_gate - jnp.sum(gate_probs * d_gate, axis=1, keepdims=True))
    d_logits = jnp.einsum("tj,tje->te", d_chosen, route_hits.astype(jnp.float32)).astype(
        jnp.bfloat16
    )
    grad_router_local = jnp.einsum(
        "td,te->de", normed_two, d_logits, preferred_element_type=jnp.float32
    )
    d_normed_two = jnp.sum(d_rows.astype(jnp.float32), axis=1) + jnp.einsum(
        "te,de->td", d_logits, router_full, preferred_element_type=jnp.float32
    )
    norm_two_out, norm_two_back = jax.vjp(rms_norm, mid_stream, gain_two)
    d_mid_norm, grad_gain_two = norm_two_back(d_normed_two)
    d_mid = cotangent + d_mid_norm
    d_attn = d_mid.astype(jnp.bfloat16)
    grad_proj_local = jnp.einsum(
        "tc,td->cd", attended_flat, d_attn, preferred_element_type=jnp.float32
    )
    d_attended = jnp.einsum(
        "td,cd->tc", d_attn, proj_full, preferred_element_type=jnp.float32
    ).astype(jnp.bfloat16)
    grad_grp = d_attended.reshape(tok_rows, KV_HEADS, groups, HEAD_DIM)
    row_delta = jnp.sum(grad_grp.astype(jnp.float32) * attended.astype(jnp.float32), axis=-1)

    def grad_step(query_grad, inputs):
        key_blk, value_blk, key_pos, key_seg = inputs
        scores = block_scores(query_grp, key_blk, positions, segments, key_pos, key_seg)
        soft_exact = jnp.exp(scores - log_total[..., None])
        soft_round = soft_exact.astype(jnp.bfloat16)
        d_soft = jnp.einsum(
            "tgrd,kgd->tgrk", grad_grp, value_blk, preferred_element_type=jnp.float32
        )
        d_scores = (soft_exact * (d_soft - row_delta[..., None])).astype(jnp.bfloat16)
        query_grad = (
            query_grad
            + jnp.einsum("tgrk,kgd->tgrd", d_scores, key_blk, preferred_element_type=jnp.float32)
            * SCORE_SCALE
        )
        d_key = (
            jnp.einsum("tgrk,tgrd->kgd", d_scores, query_grp, preferred_element_type=jnp.float32)
            * SCORE_SCALE
        )
        d_value = jnp.einsum(
            "tgrk,tgrd->kgd", soft_round, grad_grp, preferred_element_type=jnp.float32
        )
        return (
            query_grad,
            jnp.concatenate(
                [d_key.reshape(key_block, k_cols), d_value.reshape(key_block, k_cols)], axis=1
            ),
        )

    d_query, kv_terms = lax.scan(
        grad_step, start_out, (key_blocks, value_blocks, pos_blocks, seg_blocks)
    )
    d_kv = lax.psum_scatter(
        kv_terms.reshape(group_rows, 2 * k_cols), "expert", scatter_dimension=0, tiled=True
    )
    dq_pre = rotate_back(d_query.reshape(tok_rows, HEADS, HEAD_DIM), cosine_tab, sine_tab)
    dk_pre = rotate_back(
        d_kv[:, :k_cols].reshape(tok_rows, KV_HEADS, HEAD_DIM), cosine_tab, sine_tab
    )
    d_projected = jnp.concatenate(
        [dq_pre.reshape(tok_rows, q_cols), dk_pre.reshape(tok_rows, k_cols), d_kv[:, k_cols:]],
        axis=1,
    ).astype(jnp.bfloat16)
    grad_qkv_local = jnp.einsum(
        "td,tc->dc", normed_one, d_projected, preferred_element_type=jnp.float32
    )
    d_normed_one = jnp.einsum(
        "tc,dc->td", d_projected, qkv_full, preferred_element_type=jnp.float32
    )
    norm_one_out, norm_one_back = jax.vjp(rms_norm, stream_in, gain_one)
    d_in_norm, grad_gain_one = norm_one_back(d_normed_one)
    grad_in = d_mid + d_in_norm
    part_gain_one, part_qkv, part_proj, part_gain_two, part_router = (
        lax.psum_scatter(grad_gain_one, "dp", scatter_dimension=0, tiled=True),
        lax.psum_scatter(grad_qkv_local, "dp", scatter_dimension=0, tiled=True),
        lax.psum_scatter(grad_proj_local, "dp", scatter_dimension=0, tiled=True),
        lax.psum_scatter(grad_gain_two, "dp", scatter_dimension=0, tiled=True),
        lax.psum_scatter(grad_router_local, "dp", scatter_dimension=0, tiled=True),
    )
    summed = lax.psum((part_gain_one, part_qkv, part_proj, part_gain_two, part_router), "expert")
    return (
        layer_out,
        grad_in,
        summed[0],
        summed[1],
        summed[2],
        summed[3],
        summed[4],
        grad_w_in,
        grad_w_out,
    )


def solution(mesh):
    in_specs = (
        P(("dp", "expert"), None),
        P(("dp", "expert"), None),
        P("dp"),
        P("dp", None),
        P("dp", None),
        P("dp"),
        P("dp", None),
        P("expert", "dp", None),
        P("expert", None, "dp"),
        P("dp", None),
        P("dp", "expert"),
        P(("dp", "expert"), None),
    )
    out_specs = (
        P(("dp", "expert"), None),
        P(("dp", "expert"), None),
        P("dp"),
        P("dp", None),
        P("dp", None),
        P("dp"),
        P("dp", None),
        P("expert", "dp", None),
        P("expert", None, "dp"),
    )
    return jax.shard_map(local, mesh=mesh, in_specs=in_specs, out_specs=out_specs, check_vma=False)
```

profile of v0, /device:TPU:0, one launch (start us, length us, event | category | flops | bytes accessed | tf_op | source)
XLA Modules:
  0.0 1722.4 jit_solution(12972682386391190184)
XLA Ops:
  19.4 27.3 %all-gather.10.cloned.1.call-done = bf16[1024,2048]{1,0:T(8,128)(2,1)} async-done(((bf16[256,2048]{1,0:T(8,128)(2,1)}), bf16[1024,2048]{1,0:T(8,128)(2,1)}) %all-gather.10.cloned.1.call-update) | async-done | bytes 4194320 | tf_op jit(solution)/shard_map/all_gather | solution.py:121
  56.6 20.8 %all-gather = s32[1,2048]{1,0:T(1,128)S(1)} all-gather(s32[1,256]{1,0:T(1,128)S(1)} %copy-done.27), channel_id=2, replica_groups=mesh['dp'=4,'expert'=8] {'expert'}, dimensions={1}, use_global_device_ids=true | all-gather | bytes 9216 | tf_op jit(solution)/shard_map/all_gather | solution.py:152
  77.4 16.7 all-gather.2
  104.5 24.4 %all-gather.12.cloned.1.call-done = bf16[2048,1024]{1,0:T(8,128)(2,1)} async-done(((bf16[256,1024]{1,0:T(8,128)(2,1)}), bf16[2048,1024]{1,0:T(8,128)(2,1)}) %all-gather.12.cloned.1.call-update) | async-done | bytes 4194320 | tf_op jit(solution)/shard_map/all_gather | solution.py:151
  141.0 40.2 %while.37 = (s32[]{:T(128)}, f32[256,8,2]{0,2,1:T(2,128)S(1)}, f32[256,8,2]{0,2,1:T(2,128)S(1)}, s32[256]{0:T(256)S(1)}, s32[4,512]{1,0:T(4,128)S(1)}, /*index=5...) while((s32[]{:T(128)}, f32[256,8,2]{0,2,1:T(2,128)S(1)}, ...), condition=%wide.region_7.8_spmd.clone, body=%wide.region_4.7_spmd.clone.sunk | while | flops 283529216 | bytes 18446464 | solution.py:176
  192.9 20.8 %while.38 = (s32[]{:T(128)}, f32[256,8,2,64]{0,3,2,1:T(8,128)}, bf16[4,512,8,64]{1,3,2,0:T(8,128)(2,1)}, s32[256]{0:T(256)S(1)}, s32[4,512]{1,0:T(4,128)S(1)}, /...) while((s32[]{:T(128)}, f32[256,8,2,64]{0,3,2,1:T(8,128)}, ...), condition=%wide.region_9.10_spmd.clone, body=%wide.region_8.9_spmd.clone.sunk | while | flops 546177024 | bytes 3964035 | solution.py:194
  240.2 36.6 %all-gather.16.cloned.1.call-done = bf16[2,1024,1024]{2,1,0:T(8,128)(2,1)} async-done(((bf16[2,256,1024]{2,1,0:T(8,128)(2,1)}), bf16[2,1024,1024]{2,1,0:T(8,128)(2,1)}) %all-gather.16.cloned.1.call-update) | async-done | bytes 4194320 | tf_op jit(solution)/shard_map/all_gather | solution.py:129
  276.7 99.3 %all-to-all-done = bf16[8,2,192,1024]{3,2,1,0:T(8,128)(2,1)} async-done(((bf16[8,2,192,1024]{3,2,1,0:T(8,128)(2,1)}), bf16[8,2,192,1024]{3,2,1,0:T(8,128)(2,1)}, u32[]{:S(2)}, u32[]{:S(2)}) %all-to-all-start) | async-done | bytes 6291488 | tf_op jit(solution)/shard_map/all_to_all | solution.py:223
  413.6 17.2 gather_fusion.2
  431.0 114.0 %all-to-all-done.1 = bf16[8,2,192,1024]{3,2,1,0:T(8,128)(2,1)} async-done(((bf16[8,2,192,1024]{3,2,1,0:T(8,128)(2,1)}), bf16[8,2,192,1024]{3,2,1,0:T(8,128)(2,1)}, u32[]{:S(2)}, u32[]{:S(2)}) %all-to-all-start.1) | async-done | bytes 6291488 | tf_op jit(solution)/shard_map/all_to_all | solution.py:225
  545.1 14.6 gather_fusion
  578.8 142.2 %all_to_all.20 = bf16[8,2,192,1024]{3,2,1,0:T(8,128)(2,1)S(1)} all-to-all(bf16[8,2,192,1024]{3,2,1,0:T(8,128)(2,1)} %bitcast.345), channel_id=1, replica_groups=mesh['dp'=4,'expert'=8] {'expert'}, dimensions={0} | all-to-all | bytes 12582912 | tf_op jit(solution)/shard_map/all_to_all | solution.py:226
  756.1 132.4 %all-to-all-done.3 = bf16[8,2,192,1024]{3,2,1,0:T(8,128)(2,1)} async-done(((bf16[8,2,192,1024]{3,2,1,0:T(8,128)(2,1)}), bf16[8,2,192,1024]{3,2,1,0:T(8,128)(2,1)}, u32[]{:S(2)}, u32[]{:S(2)}) %all-to-all-start.3) | async-done | bytes 6291488 | tf_op jit(solution)/shard_map/all_to_all | solution.py:228
  888.5 14.9 gather_fusion.1
  913.6 241.2 %while.39 = (s32[]{:T(128)}, f32[256,8,2,64]{0,3,2,1:T(8,128)}, f32[4,512,1024]{1,0,2:T(4,128)}, bf16[4,512,8,64]{1,3,2,0:T(8,128)(2,1)}, s32[256]{0:T(256)S(1)}...) while((s32[]{:T(128)}, f32[256,8,2,64]{0,3,2,1:T(8,128)}, ...), condition=%wide.region_24.25_spmd.clone, body=%wide.region_23.24_spmd.clone.sunk | while | flops 1365114880 | bytes 75431600 | solution.py:296
  929.0 40.6 %dynamic_update_slice.6 = f32[4,512,1024]{1,0,2:T(4,128)} dynamic-update-slice(f32[4,512,1024]{1,0,2:T(4,128)} %get-tuple-element.849, f32[1,512,1024]{1,0,2:T(1,128)S(1)} %copy.233, s32[]{:T(128)} %get-tuple-element.847, s32[]{:T(128)} %constant.72.clone.1..sunk.2, s32[]{:T(128)} %constant.72.clone.1..sunk.2) | dynamic-update-slice | bytes 4194308 | tf_op jit(solution)/shard_map/while/body/jit(dynamic_update_index_in_dim)/dynamic_update_slice | solution.py:296
  988.9 40.6 %dynamic_update_slice.6 = f32[4,512,1024]{1,0,2:T(4,128)} dynamic-update-slice(f32[4,512,1024]{1,0,2:T(4,128)} %get-tuple-element.849, f32[1,512,1024]{1,0,2:T(1,128)S(1)} %copy.233, s32[]{:T(128)} %get-tuple-element.847, s32[]{:T(128)} %constant.72.clone.1..sunk.2, s32[]{:T(128)} %constant.72.clone.1..sunk.2) | dynamic-update-slice | bytes 4194308 | tf_op jit(solution)/shard_map/while/body/jit(dynamic_update_index_in_dim)/dynamic_update_slice | solution.py:296
  1049.1 40.6 %dynamic_update_slice.6 = f32[4,512,1024]{1,0,2:T(4,128)} dynamic-update-slice(f32[4,512,1024]{1,0,2:T(4,128)} %get-tuple-element.849, f32[1,512,1024]{1,0,2:T(1,128)S(1)} %copy.233, s32[]{:T(128)} %get-tuple-element.847, s32[]{:T(128)} %constant.72.clone.1..sunk.2, s32[]{:T(128)} %constant.72.clone.1..sunk.2) | dynamic-update-slice | bytes 4194308 | tf_op jit(solution)/shard_map/while/body/jit(dynamic_update_index_in_dim)/dynamic_update_slice | solution.py:296
  1109.3 40.6 %dynamic_update_slice.6 = f32[4,512,1024]{1,0,2:T(4,128)} dynamic-update-slice(f32[4,512,1024]{1,0,2:T(4,128)} %get-tuple-element.849, f32[1,512,1024]{1,0,2:T(1,128)S(1)} %copy.233, s32[]{:T(128)} %get-tuple-element.847, s32[]{:T(128)} %constant.72.clone.1..sunk.2, s32[]{:T(128)} %constant.72.clone.1..sunk.2) | dynamic-update-slice | bytes 4194308 | tf_op jit(solution)/shard_map/while/body/jit(dynamic_update_index_in_dim)/dynamic_update_slice | solution.py:296
  1170.6 142.2 %reduce-scatter.7.cloned.1.call-done = f32[256,1024]{0,1:T(8,128)} async-done(((f32[2048,1024]{0,1:T(8,128)}), f32[256,1024]{0,1:T(8,128)}) %reduce-scatter.7.cloned.1.call-update) | async-done | bytes 1048592 | tf_op jit(solution)/shard_map/reduce_scatter | solution.py:299
  1359.0 74.0 %reduce-scatter.9.cloned.1.call-done = f32[256,2048]{1,0:T(8,128)} async-done(((f32[1024,2048]{1,0:T(8,128)}), f32[256,2048]{1,0:T(8,128)}) %reduce-scatter.9.cloned.1.call-update) | async-done | bytes 2097168 | tf_op jit(solution)/shard_map/reduce_scatter | solution.py:321
  1455.6 37.7 %all-reduce.2 = (f32[256]{0:T(256)}, f32[256]{0:T(256)}, f32[256,16]{0,1:T(8,128)}) all-reduce(f32[256]{0:T(256)S(1)} %dynamic-slice.1, f32[256]{0:T(256)S(1)} %dynamic-slice.3, f32[256,16]{0,1:T(8,128)} %reduce-scatter.13.cloned.1.call-done), channel_id=1, replica_groups=mesh['dp'=4,'expert'=8] {'expert'}, use_global_device_ids=true, to_apply=%region_29.30 | all-reduce | flops 4608 | bytes 36864 | tf_op jit(solution)/shard_map/psum | solution.py:326
  1503.0 74.6 %reduce-scatter.15.cloned.1.call-done = f32[2,256,1024]{2,1,0:T(8,128)} async-done(((f32[2,1024,1024]{2,1,0:T(8,128)}), f32[2,256,1024]{2,1,0:T(8,128)}) %reduce-scatter.15.cloned.1.call-update) | async-done | bytes 2097168 | tf_op jit(solution)/shard_map/reduce_scatter | solution.py:241
  1577.6 132.3 %all-reduce.7.cloned.1.call-done = (f32[256,2048]{1,0:T(8,128)}, f32[256,1024]{1,0:T(8,128)}) async-done(((f32[256,2048]{1,0:T(8,128)}, f32[256,1024]{1,0:T(8,128)}), (f32[256,2048]{1,0:T(8,128)}, f32[256,1024]{1,0:T(8,128)})) %all-reduce.7.cloned.1.call-update) | async-done | bytes 3145744 | tf_op jit(solution)/shard_map/psum | solution.py:326
  (347 shorter events, 421.8 us)
Async XLA Ops:
  7.2 39.6 %all-gather.10.cloned.1.call-start = ((), (), s32[]{:S(2)}) async-start(), calls=%async_computation.10 | async-start | bytes 5242880 | tf_op jit(solution)/shard_map/all_gather | solution.py:121
  7.9 121.0 %all-gather.12.cloned.1.call-start = ((), (), s32[]{:S(2)}) async-start(), calls=%async_computation.11 | async-start | bytes 4718592 | tf_op jit(solution)/shard_map/all_gather | solution.py:151
  17.9 86.4 %copy-start.22 = (f32[256,64]{0,1:T(8,128)}, f32[256,64]{0,1:T(8,128)S(1)}, u32[]{:S(2)}) copy-start(f32[256,64]{0,1:T(8,128)S(1)} %get-tuple-element.547) | copy-start | bytes 196612
  17.9 86.4 %copy-start.24 = (f32[256,64]{0,1:T(8,128)}, f32[256,64]{0,1:T(8,128)S(1)}, u32[]{:S(2)}) copy-start(f32[256,64]{0,1:T(8,128)S(1)} %get-tuple-element.546) | copy-start | bytes 196612
  55.8 160.8 %all-gather.14.cloned.1.call-start = ((), (), s32[]{:S(2)}) async-start(), calls=%async_computation.12 | async-start | bytes 2621440 | tf_op jit(solution)/shard_map/all_gather | solution.py:122
  101.2 118.0 %copy-start.36 = (f32[4,1,256]{2,1,0:T(1,128)}, f32[4,1,256]{2,1,0:T(1,128)S(1)}, u32[]{:S(2)}) copy-start(f32[4,1,256]{2,1,0:T(1,128)S(1)} %convert_element_type.138) | copy-start | bytes 12292
  220.4 193.0 %copy-start.13 = (bf16[256,1024]{1,0:T(8,128)(2,1)}, bf16[256,1024]{1,0:T(8,128)(2,1)S(1)}, u32[]{:S(2)}) copy-start(bf16[256,1024]{1,0:T(8,128)(2,1)S(1)} %multiply_convert_fusion.1) | copy-start | bytes 1572868
  234.2 141.8 %all-to-all-start = ((bf16[8,2,192,1024]{3,2,1,0:T(8,128)(2,1)}), bf16[8,2,192,1024]{3,2,1,0:T(8,128)(2,1)}, u32[]{:S(2)}, u32[]{:S(2)}) async-start(bf16[8,2,192,1024]{3,2,1,0:T(8,128)(2,1)} %bitcast.344), calls=%async_computation | async-start | bytes 12582912 | tf_op jit(solution)/shard_map/all_to_all | solution.py:223
  239.0 37.7 %all-gather.16.cloned.1.call-start = ((), (), s32[]{:S(2)}) async-start(), calls=%async_computation.13 | async-start | bytes 5242880 | tf_op jit(solution)/shard_map/all_gather | solution.py:129
  239.6 153.9 %all-gather.18.cloned.1.call-start = ((), (), s32[]{:S(2)}) async-start(), calls=%async_computation.14 | async-start | bytes 2621440 | tf_op jit(solution)/shard_map/all_gather | solution.py:130
  402.9 142.2 %all-to-all-start.1 = ((bf16[8,2,192,1024]{3,2,1,0:T(8,128)(2,1)}), bf16[8,2,192,1024]{3,2,1,0:T(8,128)(2,1)}, u32[]{:S(2)}, u32[]{:S(2)}) async-start(bf16[8,2,192,1024]{3,2,1,0:T(8,128)(2,1)} %copy.158), calls=%async_computation.1 | async-start | bytes 12582912 | tf_op jit(solution)/shard_map/all_to_all | solution.py:225
  578.8 142.2 %copy-start.51 = (bf16[2,512,1024]{2,1,0:T(8,128)(2,1)S(1)}, bf16[2,512,1024]{2,1,0:T(8,128)(2,1)}, u32[]{:S(2)}) copy-start(bf16[2,512,1024]{2,1,0:T(8,128)(2,1)} %all-gather.18.cloned.1.call-done) | copy-start | bytes 6291460
  746.5 141.9 %all-to-all-start.3 = ((bf16[8,2,192,1024]{3,2,1,0:T(8,128)(2,1)}), bf16[8,2,192,1024]{3,2,1,0:T(8,128)(2,1)}, u32[]{:S(2)}, u32[]{:S(2)}) async-start(bf16[8,2,192,1024]{3,2,1,0:T(8,128)(2,1)} %copy.161), calls=%async_computation.3 | async-start | bytes 12582912 | tf_op jit(solution)/shard_map/all_to_all | solution.py:228
  751.3 561.5 %reduce-scatter.7.cloned.1.call-start = ((), (), s32[]{:S(2)}) async-start(), calls=%async_computation.15 | async-start | bytes 9437184 | tf_op jit(solution)/shard_map/reduce_scatter | solution.py:299
  1165.7 193.3 %reduce-scatter.11.cloned.1.call-start = ((), (), s32[]{:S(2)}) async-start(), calls=%async_computation.17 | async-start | bytes 5242880 | tf_op jit(solution)/shard_map/reduce_scatter | solution.py:322
  1169.6 263.4 %reduce-scatter.9.cloned.1.call-start = ((), (), s32[]{:S(2)}) async-start(), calls=%async_computation.16 | async-start | bytes 10485760 | tf_op jit(solution)/shard_map/reduce_scatter | solution.py:321
  1169.8 146.4 %copy-start.12 = (bf16[256,1024]{1,0:T(8,128)(2,1)S(1)}, bf16[256,1024]{1,0:T(8,128)(2,1)}, u32[]{:S(2)}) copy-start(bf16[256,1024]{1,0:T(8,128)(2,1)} %param.18) | copy-start | bytes 1572868
  1169.9 146.4 %copy-start.35 = (f32[4,1,256]{2,1,0:T(1,128)S(1)}, f32[4,1,256]{2,1,0:T(1,128)}, u32[]{:S(2)}) copy-start(f32[4,1,256]{2,1,0:T(1,128)} %copy-done.34) | copy-start | bytes 12292
  1169.9 146.4 %copy-start.44 = (f32[256]{0:T(256)S(1)}, f32[256]{0:T(256)}, u32[]{:S(2)}) copy-start(f32[256]{0:T(256)} %copy-done.43) | copy-start | bytes 3076
  1321.2 134.4 %reduce-scatter.13.cloned.1.call-start = ((), (), s32[]{:S(2)}) async-start(), calls=%async_computation.18 | async-start | bytes 81920 | tf_op jit(solution)/shard_map/reduce_scatter | solution.py:324
  1323.1 179.9 %reduce-scatter.17.cloned.1.call-start = ((), (), s32[]{:S(2)}) async-start(), calls=%async_computation.20 | async-start | bytes 5242880 | tf_op jit(solution)/shard_map/reduce_scatter | solution.py:242
  1332.9 244.7 %reduce-scatter.15.cloned.1.call-start = ((), (), s32[]{:S(2)}) async-start(), calls=%async_computation.19 | async-start | bytes 10485760 | tf_op jit(solution)/shard_map/reduce_scatter | solution.py:241
  1346.0 87.1 %copy-start.52 = (u32[32]{0:T(128)S(1)}, u32[32]{0:T(128)}, u32[]{:S(2)}) copy-start(u32[32]{0:T(128)} %constant.127) | copy-start | bytes 388
  1346.0 363.9 %all-reduce.7.cloned.1.call-start = ((), (), s32[]{:S(2)}) async-start(), calls=%async_computation.21 | async-start | bytes 6291456 | tf_op jit(solution)/shard_map/psum | solution.py:326
  (48 other events, 650.7 us)
Sparse Core Ops, SparseCore 0:
  9.5 37.1 all-gather.9
  56.0 72.8 all-gather.11
  130.5 21.0 all-gather.13
  241.1 35.6 all-gather.15
  278.1 22.8 all-gather.17
  1165.8 146.9 reduce-scatter.6
  1315.3 43.6 reduce-scatter.10
  1361.6 71.3 reduce-scatter.8
  1436.0 19.5 reduce-scatter.12
  1458.6 44.3 reduce-scatter.16
  1506.2 71.3 reduce-scatter.14
  1581.1 128.7 all-reduce.6
where the time goes:
time: 1730 us; the launch traced here: 1720 us
  waiting for transfers between devices  891 us (52%)
  local copies, waits for them, and re-layouts  310 us (18%)
  blocking collectives  240 us (14%)
  matrix products  186 us (11%)
  other arithmetic  64.1 us (4%)
    dynamic_update_slice x8, local copies, waits for them, and re-layouts, local(): lax.scan(grad_step, start_out, (key_blocks, value_blocks, pos_blocks, seg...  171 us
    all_to_all x1, blocking collectives, local(): lax.all_to_all(d_outgoing, 'expert', split_axis=0, concat_axis=0, tiled=T...  142 us
    reduce_scatter x1, waiting for transfers between devices, local(): lax.psum_scatter(kv_terms.reshape(group_rows, 2 * k_cols), 'expert', scat...  142 us
    all_to_all x1, waiting for transfers between devices, local(): lax.all_to_all(d_slots, 'expert', split_axis=0, concat_axis=0, tiled=True)  132 us
    psum x1, waiting for transfers between devices, local(): lax.psum((part_gain_one, part_qkv, part_proj, part_gain_two, part_router)...  132 us
    all_to_all x1, waiting for transfers between devices, local(): lax.all_to_all(produced, 'expert', split_axis=0, concat_axis=0, tiled=True)  114 us
    all_to_all x1, waiting for transfers between devices, local(): lax.all_to_all(outgoing, 'expert', split_axis=0, concat_axis=0, tiled=True)  99.3 us
    reduce_scatter x1, waiting for transfers between devices, local(): lax.psum_scatter(grad_in_local, 'dp', scatter_dimension=1, tiled=True)  74.6 us
  transfers between devices with their start and end apart: 15, of which 13 were waited for; matrix products, arithmetic and copies ran while one was open for 10% of the time, Pallas kernels for 0%

commit v1 on v0

v1 whole, which is shorter than its diff:
```python
import jax
import jax.numpy as jnp
from jax import lax
from jax.experimental import pallas as pl
from jax.experimental.pallas import tpu as pltpu
from jax.sharding import PartitionSpec as P

HEADS = 16
KV_HEADS = 8
HEAD_DIM = 64
GROUPS = HEADS // KV_HEADS
EPSILON = 1e-06
ROPE_BASE = 10000.0
SCORE_SCALE = 0.015625
MASKED = -1e30
F32 = jnp.float32
BF16 = jnp.bfloat16
Q_TILE = 256
K_TILE = 256


def rms_norm(values, gain_vec):
    factor = lax.rsqrt(jnp.mean(values * values, axis=-1, keepdims=True) + EPSILON)
    return values * factor * gain_vec


def dot(left, right, left_dim=1, right_dim=0):
    return lax.dot_general(
        left, right, (((left_dim,), (right_dim,)), ((), ())), preferred_element_type=F32
    )


def rotate(values, cosine, sine):
    half = HEAD_DIM // 2
    one, two = values[:half], values[half:]
    return jnp.concatenate([one * cosine - two * sine, two * cosine + one * sine], axis=0)


def rotate_back(grads, cosine, sine):
    half = HEAD_DIM // 2
    one, two = grads[:half], grads[half:]
    return jnp.concatenate([one * cosine + two * sine, two * cosine - one * sine], axis=0)


def attend_kernel(low, high, key_pos, query, key, value_t, out, lse, score_buf, weight_buf):
    heads = query.shape[0]
    low_row, high_row = low[...], high[...]
    steps = key.shape[0] // K_TILE

    def score_step(step, maxima):
        rows = pl.ds(pl.multiple_of(step * K_TILE, K_TILE), K_TILE)
        at = key_pos[rows, :]
        allowed = (at >= low_row) & (at <= high_row)
        found = []
        for head in range(heads):
            scores = jnp.dot(key[rows, :], query[head], preferred_element_type=F32)
            scores = jnp.where(allowed, scores, MASKED)
            score_buf[head, rows, :] = scores
            found.append(jnp.maximum(maxima[head], jnp.max(scores, axis=0, keepdims=True)))
        return tuple(found)

    start = tuple(jnp.full(low_row.shape, MASKED, F32) for _ in range(heads))
    maxima = lax.fori_loop(0, steps, score_step, start)

    def weight_step(step, totals):
        rows = pl.ds(pl.multiple_of(step * K_TILE, K_TILE), K_TILE)
        found = []
        for head in range(heads):
            weights = jnp.exp(score_buf[head, rows, :] - maxima[head])
            weight_buf[head, rows, :] = weights.astype(BF16)
            found.append(totals[head] + jnp.sum(weights, axis=0, keepdims=True))
        return tuple(found)

    start = tuple(jnp.zeros(low_row.shape, F32) for _ in range(heads))
    totals = lax.fori_loop(0, steps, weight_step, start)
    for head in range(heads):
        summed = jnp.dot(value_t[...], weight_buf[head], preferred_element_type=F32)
        out[head] = (summed / totals[head]).astype(BF16)
        lse[head] = maxima[head] + jnp.log(totals[head])


def attend(low, high, key_pos, query, key, value_t):
    heads, width, rows = query.shape
    tile = low_tile(rows)
    whole = lambda i: (0, 0)
    lane = lambda i: (0, i)
    return pl.pallas_call(
        attend_kernel,
        grid=(rows // tile,),
        in_specs=[
            pl.BlockSpec((1, tile), lane),
            pl.BlockSpec((1, tile), lane),
            pl.BlockSpec((rows, tile), whole),
            pl.BlockSpec((heads, width, tile), lambda i: (0, 0, i)),
            pl.BlockSpec((rows, width), whole),
            pl.BlockSpec((width, rows), whole),
        ],
        out_specs=[
            pl.BlockSpec((heads, width, tile), lambda i: (0, 0, i)),
            pl.BlockSpec((heads, 1, tile), lambda i: (0, 0, i)),
        ],
        out_shape=[
            jax.ShapeDtypeStruct((heads, width, rows), BF16),
            jax.ShapeDtypeStruct((heads, 1, rows), F32),
        ],
        scratch_shapes=[
            pltpu.VMEM((heads, rows, tile), F32),
            pltpu.VMEM((heads, rows, tile), BF16),
        ],
        cost_estimate=pl.CostEstimate(
            flops=4 * heads * rows * rows * 256,
            bytes_accessed=8 * rows * 256,
            transcendentals=heads * rows * rows,
        ),
        name="attend",
    )(low, high, key_pos, query, key, value_t)


def low_tile(rows):
    return min(Q_TILE, rows)


def attend_back_kernel(
    low, high, key_pos, query, query_n, key, key_t, value, grad, grad_n, lse, delta,
    d_query, d_key, d_value, score_buf,
):
    heads = query.shape[0]
    low_row, high_row = low[...], high[...]
    steps = key.shape[0] // K_TILE

    @pl.when(pl.program_id(0) == 0)
    def _():
        d_key[...] = jnp.zeros_like(d_key)
        d_value[...] = jnp.zeros_like(d_value)

    @pl.loop(0, steps)
    def _(step):
        rows = pl.ds(pl.multiple_of(step * K_TILE, K_TILE), K_TILE)
        at = key_pos[rows, :]
        allowed = (at >= low_row) & (at <= high_row)
        key_sum, value_sum = d_key[rows, :], d_value[rows, :]
        for head in range(heads):
            scores = jnp.dot(key[rows, :], query[head], preferred_element_type=F32)
            weights = jnp.exp(jnp.where(allowed, scores - lse[head], MASKED))
            d_soft = jnp.dot(value[rows, :], grad[head], preferred_element_type=F32)
            d_scores = (weights * (d_soft - delta[head])).astype(BF16)
            score_buf[head, rows, :] = d_scores
            key_sum += jnp.dot(d_scores, query_n[head], preferred_element_type=F32)
            value_sum += jnp.dot(weights.astype(BF16), grad_n[head], preferred_element_type=F32)
        d_key[rows, :] = key_sum
        d_value[rows, :] = value_sum

    for head in range(heads):
        d_query[head] = jnp.dot(key_t[...], score_buf[head], preferred_element_type=F32)


def attend_back(
    low, high, key_pos, query, query_n, key, key_t, value, grad, grad_n, lse, delta
):
    heads, width, rows = query.shape
    tile = low_tile(rows)
    whole = lambda i: (0, 0)
    lane = lambda i: (0, i)
    wide = pl.BlockSpec((heads, width, tile), lambda i: (0, 0, i))
    tall = pl.BlockSpec((heads, tile, width), lambda i: (0, i, 0))
    row = pl.BlockSpec((heads, 1, tile), lambda i: (0, 0, i))
    keys = pl.BlockSpec((rows, width), whole)
    return pl.pallas_call(
        attend_back_kernel,
        grid=(rows // tile,),
        in_specs=[
            pl.BlockSpec((1, tile), lane),
            pl.BlockSpec((1, tile), lane),
            pl.BlockSpec((rows, tile), whole),
            wide, tall, keys, pl.BlockSpec((width, rows), whole), keys, wide, tall, row, row,
        ],
        out_specs=[wide, keys, keys],
        out_shape=[
            jax.ShapeDtypeStruct((heads, width, rows), F32),
            jax.ShapeDtypeStruct((rows, width), F32),
            jax.ShapeDtypeStruct((rows, width), F32),
        ],
        scratch_shapes=[pltpu.VMEM((heads, rows, tile), BF16)],
        cost_estimate=pl.CostEstimate(
            flops=10 * heads * rows * rows * 256,
            bytes_accessed=8 * rows * 256,
            transcendentals=heads * rows * rows,
        ),
        name="attend_back",
    )(low, high, key_pos, query, query_n, key, key_t, value, grad, grad_n, lse, delta)


def gather(values, name, axis=0):
    return lax.all_gather(values, name, axis=axis, tiled=True)


def exchange(values, name="expert"):
    return lax.all_to_all(values, name, split_axis=0, concat_axis=0, tiled=True)


def give_back(partial):
    return lax.psum_scatter(
        partial.astype(BF16), "expert", scatter_dimension=0, tiled=True
    ).astype(F32)


def local(
    hidden_in, d_out, gain_attn, w_qkv, w_o, gain_moe, w_router, w_in, w_out,
    seq_lengths, assign, routes,
):
    tok_rows, width = hidden_in.shape
    exp_dev, _, ff_two = w_in.shape
    ff = ff_two // 2
    n_expert = lax.axis_size("expert")
    me = lax.axis_index("expert")
    experts = exp_dev * n_expert
    group_rows = tok_rows * n_expert
    q_per = HEADS // n_expert
    share = GROUPS // q_per
    q_cols = q_per * HEAD_DIM
    k_base = HEADS * HEAD_DIM
    v_base = k_base + KV_HEADS * HEAD_DIM
    cols = q_cols + 2 * HEAD_DIM

    pack = gather(
        jnp.concatenate([gain_attn[None], gain_moe[None], w_router.T], axis=0), "dp", axis=1
    )
    gain_one, gain_two = pack[0].astype(F32), pack[1].astype(F32)
    router_t = pack[2:]
    kv_head = (me * q_per) // GROUPS
    w_heads = gather(
        jnp.concatenate(
            [
                lax.dynamic_slice_in_dim(w_qkv, me * q_cols, q_cols, 1),
                lax.dynamic_slice_in_dim(w_qkv, k_base + kv_head * HEAD_DIM, HEAD_DIM, 1),
                lax.dynamic_slice_in_dim(w_qkv, v_base + kv_head * HEAD_DIM, HEAD_DIM, 1),
            ],
            axis=1,
        ),
        "dp",
    )
    stream_in = hidden_in.astype(F32)
    normed_one = rms_norm(stream_in, gain_one).astype(BF16)
    normed_all = gather(normed_one, "expert")
    position = gather(assign[0], "expert")
    proj_full = gather(w_o, "dp")
    weight_in = gather(w_in, "dp", axis=1)
    d_out_all = gather(d_out, "expert")
    routes_all = gather(routes, "expert")
    weight_out = gather(w_out, "dp", axis=2)
    pieces = []
    for dev in range(n_expert):
        head = (dev * q_per) // GROUPS * HEAD_DIM
        pieces += [
            w_qkv[:, dev * q_cols : (dev + 1) * q_cols],
            w_qkv[:, k_base + head : k_base + head + HEAD_DIM],
            w_qkv[:, v_base + head : v_base + head + HEAD_DIM],
        ]
    qkv_full = gather(jnp.concatenate(pieces, axis=1), "dp")

    lengths = seq_lengths[0]
    ends = jnp.cumsum(lengths)
    starts = ends - lengths
    seq_id = jnp.sum((position[None, :] >= ends[:, None]).astype(jnp.int32), axis=0)
    picks = seq_id[None, :] == jnp.arange(lengths.shape[0], dtype=jnp.int32)[:, None]
    start_of = jnp.sum(jnp.where(picks, starts[:, None], 0), axis=0)
    rot_pos = position - start_of
    half = HEAD_DIM // 2
    frequency = ROPE_BASE ** (-(jnp.arange(half).astype(F32) * (2.0 / HEAD_DIM)))
    angles = frequency[:, None] * rot_pos.astype(F32)[None, :]
    cosine, sine = jnp.cos(angles), jnp.sin(angles)
    low, high = start_of[None, :], position[None, :]
    key_pos = jnp.broadcast_to(position[:, None], (group_rows, low_tile(group_rows)))

    projected = dot(w_heads, normed_all, 0, 1)
    query = jnp.stack(
        [
            rotate(projected[h * HEAD_DIM : (h + 1) * HEAD_DIM], cosine, sine).astype(BF16)
            for h in range(q_per)
        ]
    ) * jnp.asarray(SCORE_SCALE, BF16)
    key_t = rotate(projected[q_cols : q_cols + HEAD_DIM], cosine, sine).astype(BF16)
    value_t = projected[q_cols + HEAD_DIM :].astype(BF16)
    key, value = key_t.T, value_t.T
    heads_out, lse = attend(low, high, key_pos, query, key, value_t)
    attended_t = heads_out.reshape(q_cols, group_rows)
    attended = exchange(attended_t.T.reshape(n_expert, tok_rows, q_cols))
    attended = attended.transpose(1, 0, 2).reshape(tok_rows, HEADS * HEAD_DIM)
    mid_stream = stream_in + dot(attended, proj_full)
    normed_two = rms_norm(mid_stream, gain_two).astype(BF16)

    rows_all = gather(normed_two, "expert")
    named = jnp.any(
        routes_all[:, :, None] == jnp.arange(experts, dtype=jnp.int32)[None, None, :], axis=1
    )
    gates = jax.nn.softmax(jnp.where(named, dot(rows_all, router_t, 1, 1), -jnp.inf), axis=1)
    mine = lax.dynamic_slice_in_dim(gates, me * exp_dev, exp_dev, 1)
    made, d_rows, gate_cols, grads_in, grads_out = 0.0, 0.0, [], [], []
    for one in range(exp_dev):
        weight = mine[:, one : one + 1]
        d_plain = dot(d_out_all, weight_out[one], 1, 1)
        gate_up = dot(rows_all, weight_in[one])
        gate_pre, up_pre = gate_up[:, :ff], gate_up[:, ff:]
        sigmoid = jax.nn.sigmoid(gate_pre)
        active = gate_pre * sigmoid
        hidden = active * up_pre
        gate_cols.append(jnp.sum(hidden * d_plain, axis=1))
        scaled = (weight * hidden).astype(BF16)
        d_hidden = weight * d_plain
        d_gate_up = jnp.concatenate(
            [
                d_hidden * up_pre * sigmoid * (1.0 + gate_pre * (1.0 - sigmoid)),
                d_hidden * active,
            ],
            axis=1,
        ).astype(BF16)
        d_rows = d_rows + dot(d_gate_up, weight_in[one], 1, 1)
        made = made + dot(scaled, weight_out[one])
        grads_out.append(dot(scaled, d_out_all, 0, 0))
        grads_in.append(dot(rows_all, d_gate_up, 0, 0))
    d_gate = exchange(
        jnp.stack(gate_cols).reshape(exp_dev, n_expert, tok_rows).transpose(1, 0, 2)
    )
    d_gate = d_gate.reshape(experts, tok_rows).T
    d_back = give_back(d_rows)
    moe_sum = give_back(made)
    layer_out = (mid_stream + moe_sum).astype(BF16)
    grad_w_in = lax.psum_scatter(jnp.stack(grads_in), "dp", scatter_dimension=1, tiled=True)
    grad_w_out = lax.psum_scatter(jnp.stack(grads_out), "dp", scatter_dimension=2, tiled=True)

    own_gates = lax.dynamic_slice_in_dim(gates, me * tok_rows, tok_rows, 0)
    d_logits = (
        own_gates * (d_gate - jnp.sum(own_gates * d_gate, axis=1, keepdims=True))
    ).astype(BF16)
    grad_router = dot(d_logits, normed_two, 0, 0)
    d_normed_two = d_back + dot(d_logits, router_t)
    _, norm_two_back = jax.vjp(rms_norm, mid_stream, gain_two)
    d_mid_norm, grad_gain_two = norm_two_back(d_normed_two)
    d_mid = d_out.astype(F32) + d_mid_norm

    d_attn_all = gather(d_mid.astype(BF16), "expert")
    w_o_mine = lax.dynamic_slice_in_dim(proj_full, me * q_cols, q_cols, 0)
    d_heads = dot(w_o_mine, d_attn_all, 1, 1).astype(BF16).reshape(q_per, HEAD_DIM, group_rows)
    delta = jnp.sum(d_heads.astype(F32) * heads_out.astype(F32), axis=1, keepdims=True)
    d_query, d_key, d_value = attend_back(
        low, high, key_pos, query, jnp.swapaxes(query, 1, 2), key, key_t, value,
        d_heads, jnp.swapaxes(d_heads, 1, 2), lse, delta,
    )
    d_projected = jnp.concatenate(
        [rotate_back(d_query[h] * SCORE_SCALE, cosine, sine) for h in range(q_per)]
        + [rotate_back(d_key.T, cosine, sine), d_value.T],
        axis=0,
    ).astype(BF16)
    d_projected = d_projected.T
    d_own = exchange(d_projected.reshape(n_expert, tok_rows, cols))
    d_own = d_own.transpose(1, 0, 2).reshape(tok_rows, n_expert * cols)
    d_normed_one = dot(d_own, qkv_full, 1, 1)
    _, norm_one_back = jax.vjp(rms_norm, stream_in, gain_one)
    d_in_norm, grad_gain_one = norm_one_back(d_normed_one)
    grad_in = d_mid + d_in_norm

    part_o = lax.psum_scatter(
        dot(attended_t, d_attn_all), "dp", scatter_dimension=1, tiled=True
    )
    grad_w_o = lax.all_to_all(
        gather(part_o, "expert"), "dp", split_axis=0, concat_axis=1, tiled=True
    )
    part_qkv = lax.psum_scatter(
        dot(normed_all, d_projected, 0, 0), "dp", scatter_dimension=0, tiled=True
    )
    joined = lax.all_gather(part_qkv, "expert", axis=0)

    def columns(stack):
        return stack.transpose(1, 0, 2).reshape(stack.shape[1], -1)

    def shared(stack):
        return columns(stack.reshape((KV_HEADS, share) + stack.shape[1:]).sum(axis=1))

    grad_w_qkv = jnp.concatenate(
        [
            columns(joined[:, :, :q_cols]),
            shared(joined[:, :, q_cols : q_cols + HEAD_DIM]),
            shared(joined[:, :, q_cols + HEAD_DIM :]),
        ],
        axis=1,
    )
    small = jnp.concatenate([grad_gain_one[None], grad_gain_two[None], grad_router], axis=0)
    small = lax.psum(
        lax.psum_scatter(small, "dp", scatter_dimension=1, tiled=True), "expert"
    )
    return (
        layer_out, grad_in, small[0], grad_w_qkv, grad_w_o, small[1], small[2:].T,
        grad_w_in, grad_w_out,
    )


def solution(mesh):
    rows = P(("dp", "expert"), None)
    in_specs = (
        rows, rows, P("dp"), P("dp", None), P("dp", None), P("dp"), P("dp", None),
        P("expert", "dp", None), P("expert", None, "dp"), P("dp", None), P("dp", "expert"), rows,
    )
    out_specs = (
        rows, rows, P("dp"), P("dp", None), P("dp", None), P("dp"), P("dp", None),
        P("expert", "dp", None), P("expert", None, "dp"),
    )
    return jax.shard_map(local, mesh=mesh, in_specs=in_specs, out_specs=out_specs, check_vma=False)
```

time: 1730 us -> 1010 us (0.58)
  waiting for transfers between devices: 891 us -> 595 us
  local copies, waits for them, and re-layouts: 310 us -> 44.8 us
  blocking collectives: 240 us -> 123 us
  matrix products: 186 us -> 107 us
  Pallas kernels: 0 us -> 72 us
  other arithmetic: 64.1 us -> 29.9 us
    all_to_all x3, waiting for transfers between devices: 346 us -> 34.6 us  [the longest x2 34.6 us: exchange(): return lax.all_to_all(values, name, split_axis=0, concat_axis=0, tiled=True)]
    all_gather x5 -> x10, waiting for transfers between devices: 88.3 us -> 274 us  [the longest x9 265 us: gather(): return lax.all_gather(values, name, axis=axis, tiled=True)]
    dynamic_update_slice x8 -> x0, local copies, waits for them, and re-layouts: 171 us -> none  [local(): lax.scan(grad_step, start_out, (key_blocks, value_blocks, pos_blocks, seg...]
    psum x1 -> x0, waiting for transfers between devices: 132 us -> none  [local(): lax.psum((part_gain_one, part_qkv, part_proj, part_gain_two, part_router)...]
    all_to_all x1, blocking collectives: 142 us -> 17.6 us  [exchange(): return lax.all_to_all(values, name, split_axis=0, concat_axis=0, tiled=True)]
    dot_general x45 -> x21, matrix products: 186 us -> 107 us  [dot(): lax.dot_general(left, right, (((left_dim,), (right_dim,)), ((), ())), pre...]
    pallas_call x0 -> x2, Pallas kernels: none -> 72 us  [the longest x1 45.4 us: attend_back(): pl.pallas_call(attend_back_kernel, grid=(rows // tile,), in_specs=[pl.Blo...]
    gather x7 -> x0, local copies, waits for them, and re-layouts: 47 us -> none  [the longest x5 17.6 us: local(): jnp.take_along_axis(logits, routes, axis=1)]
  transfers between devices with their start and end apart: 15 -> 20, of which waited for: 13 -> 14; matrix products, arithmetic and copies ran while one was open for 10% -> 13% of each run, Pallas kernels for 0% -> 7%
where the time goes in v1:
time: 1010 us; the launch traced here: 1000 us
  waiting for transfers between devices  595 us (59%)
  blocking collectives  123 us (12%)
  matrix products  107 us (11%)
  Pallas kernels  72 us (7%)
  local copies, waits for them, and re-layouts  44.8 us (4%)
  other arithmetic  29.9 us (3%)
  between operations  15.1 us (1%)
  starting transfers between devices  13 us (1%)
    all_gather x9, waiting for transfers between devices, gather(): return lax.all_gather(values, name, axis=axis, tiled=True)  265 us
    reduce_scatter x2, waiting for transfers between devices, give_back(): lax.psum_scatter(partial.astype(BF16), 'expert', scatter_dimension=0, til...  150 us
    dot_general x21, matrix products, dot(): lax.dot_general(left, right, (((left_dim,), (right_dim,)), ((), ())), pre...  107 us
    reduce_scatter x1, waiting for transfers between devices, local(): lax.psum_scatter(jnp.stack(grads_in), 'dp', scatter_dimension=1, tiled=True)  74.4 us
    all_gather x4, blocking collectives, gather(): return lax.all_gather(values, name, axis=axis, tiled=True)  66.6 us
    pallas_call x1, Pallas kernels, attend_back(): pl.pallas_call(attend_back_kernel, grid=(rows // tile,), in_specs=[pl.Blo...  45.4 us
    reduce_scatter x1, waiting for transfers between devices, local(): lax.psum_scatter(jnp.stack(grads_out), 'dp', scatter_dimension=2, tiled=T...  40 us
    psum x1, blocking collectives, local(): lax.psum(lax.psum_scatter(small, 'dp', scatter_dimension=1, tiled=True),...  38.4 us
  transfers between devices with their start and end apart: 20, of which 14 were waited for; matrix products, arithmetic and copies ran while one was open for 13% of the time, Pallas kernels for 7%

profile of v1, /device:TPU:0, one launch (start us, length us, event | category | flops | bytes accessed | tf_op | source)
XLA Modules:
  0.0 1000.0 jit_solution(18411480033458756811)
XLA Ops:
  22.8 7.6 all_gather.46
  30.5 21.4 %all-gather.high = s32[1,2048]{1,0:T(1,128)S(1)} all-gather(s32[1,256]{1,0:T(1,128)S(1)} %copy-done.23), channel_id=2, replica_groups=mesh['dp'=4,'expert'=8] {'expert'}, dimensions={1}, use_global_device_ids=true | all-gather | bytes 9216 | tf_op jit(solution)/shard_map/all_gather | solution.py:194
  52.3 41.4 %all-gather.13.cloned.1.call-done = bf16[2048,1024]{1,0:T(8,128)(2,1)} async-done(((bf16[256,1024]{1,0:T(8,128)(2,1)}), bf16[2048,1024]{1,0:T(8,128)(2,1)}) %all-gather.13.cloned.1.call-update) | async-done | bytes 4194320 | tf_op jit(solution)/shard_map/all_gather | solution.py:194
  104.2 26.6 %attend.1 = (bf16[2,64,2048]{2,1,0:T(8,128)(2,1)}, f32[2,1,2048]{2,1,0:T(1,128)}) custom-call(s32[1,2048]{1,0:T(1,128)} %bitcast.185, s32[1,2048]{1,0:T(1,128)} %copy-done.8, s32[2048,256]{1,0:T(8,128)} %broadcast_in_dim.36.key_pos, bf16[2,64,2048]{2,1,0:T(8,128)(2,1)} %get-tuple-element.77.query, bf16[2048,64]{1,0:T(8,128)(2,1)} %copy.85.key, ...), custom_call_target="tpu_custom_call" | custom-call | flops 8589934592 | bytes 4194304 | tf_op jit(solution)/shard_map/attend/pallas_call | solution.py:87
  132.1 17.6 %all_to_all.34 = bf16[8,256,128]{2,1,0:T(8,128)(2,1)S(1)} all-to-all(bf16[8,256,128]{2,1,0:T(8,128)(2,1)S(1)} %bitcast.169), channel_id=1, replica_groups=mesh['dp'=4,'expert'=8] {'expert'}, dimensions={0} | all-to-all | bytes 1048576 | tf_op jit(solution)/shard_map/all_to_all | solution.py:198
  155.2 31.4 %all_gather.50 = s32[2048,8]{0,1:T(8,128)S(1)} all-gather(s32[256,8]{0,1:T(8,128)S(1)} %copy-done.21), channel_id=1, replica_groups=mesh['dp'=4,'expert'=8] {'expert'}, dimensions={0}, use_global_device_ids=true | all-gather | bytes 73728 | tf_op jit(solution)/shard_map/all_gather | solution.py:194
  186.7 39.0 %all-gather.17.cloned.1.call-done = bf16[2048,1024]{1,0:T(8,128)(2,1)} async-done(((bf16[256,1024]{1,0:T(8,128)(2,1)}), bf16[2048,1024]{1,0:T(8,128)(2,1)}) %all-gather.17.cloned.1.call-update) | async-done | bytes 4194320 | tf_op jit(solution)/shard_map/all_gather | solution.py:194
  229.3 30.9 %all-gather.19.cloned.1.call-done = bf16[2,1024,1024]{2,1,0:T(8,128)(2,1)} async-done(((bf16[2,256,1024]{2,1,0:T(8,128)(2,1)}), bf16[2,1024,1024]{2,1,0:T(8,128)(2,1)}) %all-gather.19.cloned.1.call-update) | async-done | bytes 4194320 | tf_op jit(solution)/shard_map/all_gather | solution.py:194
  260.2 10.8 %fusion.7 = f32[2048,1024]{0,1:T(8,128)} fusion(bf16[2048,1024]{1,0:T(8,128)(2,1)} %all-gather.17.cloned.1.call-done, bf16[2,1024,1024]{2,1,0:T(8,128)(2,1)} %all-gather.19.cloned.1.call-done), kind=kOutput, calls=%fused_computation.35 | convolution fusion | flops 4294967296 | bytes 14680064 | tf_op jit(solution)/shard_map/dot_general | solution.py:28
  271.0 7.5 fusion.8
  284.5 74.8 %all-gather.23.cloned.1.call-done = bf16[2048,1024]{1,0:T(8,128)(2,1)} async-done(((bf16[256,1024]{1,0:T(8,128)(2,1)}), bf16[2048,1024]{1,0:T(8,128)(2,1)}) %all-gather.23.cloned.1.call-update) | async-done | bytes 4194320 | tf_op jit(solution)/shard_map/all_gather | solution.py:194
  359.3 9.4 multiply_convert_fusion.3
  380.4 9.1 add_convert_fusion
  400.2 76.3 %reduce-scatter.10.cloned.1.call-done = bf16[256,1024]{1,0:T(8,128)(2,1)} async-done(((bf16[2048,1024]{1,0:T(8,128)(2,1)}), bf16[256,1024]{1,0:T(8,128)(2,1)}) %reduce-scatter.10.cloned.1.call-update) | async-done | bytes 524304 | tf_op jit(solution)/shard_map/reduce_scatter | solution.py:202
  481.6 72.5 %all-gather.25.cloned.1.call-done = bf16[2048,1024]{1,0:T(8,128)(2,1)} async-done(((bf16[256,1024]{1,0:T(8,128)(2,1)}), bf16[2048,1024]{1,0:T(8,128)(2,1)}) %all-gather.25.cloned.1.call-update) | async-done | bytes 4194320 | tf_op jit(solution)/shard_map/all_gather | solution.py:194
  571.3 45.4 %attend_back.1 = (f32[2,64,2048]{2,1,0:T(8,128)}, f32[2048,64]{1,0:T(8,128)}, f32[2048,64]{1,0:T(8,128)}) custom-call(s32[1,2048]{1,0:T(1,128)} %bitcast.186, s32[1,2048]{1,0:T(1,128)} %copy-done.8, s32[2048,256]{1,0:T(8,128)} %broadcast_in_dim.36.key_pos, bf16[2,64,2048]{2,1,0:T(8,128)(2,1)} %get-tuple-element.77.query, bf16[2,2048,64]{2,1,0:T(8,128)(2,1)} %copy.90.query_n, ...), custom_call_target="tpu_custom_call" | custom-call | flops 21474836480 | bytes 4194304 | tf_op jit(solution)/shard_map/attend_back/pallas_call | solution.py:168
  659.3 28.0 %all-to-all-done.2 = bf16[8,256,256]{1,2,0:T(8,128)(2,1)} async-done(((bf16[8,256,256]{1,2,0:T(8,128)(2,1)}), bf16[8,256,256]{1,2,0:T(8,128)(2,1)}, u32[]{:S(2)}, u32[]{:S(2)}) %all-to-all-start.2) | async-done | bytes 1048608 | tf_op jit(solution)/shard_map/all_to_all | solution.py:198
  703.8 8.3 fusion.5
  725.8 74.1 %reduce-scatter.8.cloned.1.call-done = bf16[256,1024]{1,0:T(8,128)(2,1)} async-done(((bf16[2048,1024]{1,0:T(8,128)(2,1)}), bf16[256,1024]{1,0:T(8,128)(2,1)}) %reduce-scatter.8.cloned.1.call-update) | async-done | bytes 524304 | tf_op jit(solution)/shard_map/reduce_scatter | solution.py:202
  802.9 18.5 %reduce-scatter.12.cloned.1.call-done = f32[18,256]{1,0:T(8,128)} async-done(((f32[18,1024]{1,0:T(8,128)}), f32[18,256]{1,0:T(8,128)}) %reduce-scatter.12.cloned.1.call-update) | async-done | bytes 18448 | tf_op jit(solution)/shard_map/reduce_scatter | solution.py:389
  821.4 38.4 %psum.7 = f32[18,256]{1,0:T(8,128)S(1)} all-reduce(f32[18,256]{1,0:T(8,128)} %reduce-scatter.12.cloned.1.call-done), channel_id=1, replica_groups=mesh['dp'=4,'expert'=8] {'expert'}, use_global_device_ids=true, to_apply=%region_19.20 | all-reduce | flops 4608 | bytes 36864 | tf_op jit(solution)/shard_map/psum | solution.py:388
  863.3 9.3 all-gather.31.cloned.1.call-done
  878.5 40.0 %reduce-scatter.20.cloned.1.call-done = f32[2,512,256]{2,1,0:T(8,128)} async-done(((f32[2,512,1024]{2,1,0:T(8,128)}), f32[2,512,256]{2,1,0:T(8,128)}) %reduce-scatter.20.cloned.1.call-update) | async-done | bytes 1048592 | tf_op jit(solution)/shard_map/reduce_scatter | solution.py:329
  918.6 74.4 %reduce-scatter.18.cloned.1.call-done = f32[2,256,1024]{2,1,0:T(8,128)} async-done(((f32[2,1024,1024]{2,1,0:T(8,128)}), f32[2,256,1024]{2,1,0:T(8,128)}) %reduce-scatter.18.cloned.1.call-update) | async-done | bytes 2097168 | tf_op jit(solution)/shard_map/reduce_scatter | solution.py:328
  (207 shorter events, 172.1 us)
Async XLA Ops:
  7.2 86.4 %all-gather.13.cloned.1.call-start = ((), (), s32[]{:S(2)}) async-start(), calls=%async_computation.11 | async-start | bytes 4718592 | tf_op jit(solution)/shard_map/all_gather | solution.py:194
  18.9 131.1 %all-gather.15.cloned.1.call-start = ((), (), s32[]{:S(2)}) async-start(), calls=%async_computation.12 | async-start | bytes 2621440 | tf_op jit(solution)/shard_map/all_gather | solution.py:194
  19.7 206.1 %all-gather.17.cloned.1.call-start = ((), (), s32[]{:S(2)}) async-start(), calls=%async_computation.13 | async-start | bytes 4718592 | tf_op jit(solution)/shard_map/all_gather | solution.py:194
  153.4 106.8 %all-gather.19.cloned.1.call-start = ((), (), s32[]{:S(2)}) async-start(), calls=%async_computation.14 | async-start | bytes 5242880 | tf_op jit(solution)/shard_map/all_gather | solution.py:194
  154.0 130.4 %all-gather.21.cloned.1.call-start = ((), (), s32[]{:S(2)}) async-start(), calls=%async_computation.15 | async-start | bytes 2621440 | tf_op jit(solution)/shard_map/all_gather | solution.py:194
  154.6 204.7 %all-gather.23.cloned.1.call-start = ((), (), s32[]{:S(2)}) async-start(), calls=%async_computation.17 | async-start | bytes 4718592 | tf_op jit(solution)/shard_map/all_gather | solution.py:194
  155.2 321.3 %reduce-scatter.10.cloned.1.call-start = ((), (), s32[]{:S(2)}) async-start(), calls=%async_computation.18 | async-start | bytes 4718592 | tf_op jit(solution)/shard_map/reduce_scatter | solution.py:202
  389.5 164.6 %copy-start.4 = (bf16[2,64,2048]{2,1,0:T(8,128)(2,1)S(1)}, bf16[2,64,2048]{2,1,0:T(8,128)(2,1)}, u32[]{:S(2)}) copy-start(bf16[2,64,2048]{2,1,0:T(8,128)(2,1)} %get-tuple-element.14) | copy-start | bytes 1572868
  390.1 10.0 %all-to-all-start.1 = ((f32[8,2,256]{2,1,0:T(2,128)}), f32[8,2,256]{2,1,0:T(2,128)S(1)}, u32[]{:S(2)}, u32[]{:S(2)}) async-start(f32[8,2,256]{2,1,0:T(2,128)} %maximum_bitcast_fusion), calls=%async_computation.3 | async-start | bytes 32768 | tf_op jit(solution)/shard_map/all_to_all | solution.py:198
  393.5 160.6 %all-gather.25.cloned.1.call-start = ((), (), s32[]{:S(2)}) async-start(), calls=%async_computation.19 | async-start | bytes 4718592 | tf_op jit(solution)/shard_map/all_gather | solution.py:194
  479.3 78.5 %copy-start.17 = (f32[256]{0:T(256)}, f32[256]{0:T(256)S(1)}, u32[]{:S(2)}) copy-start(f32[256]{0:T(256)S(1)} %multiply_multiply_fusion.1) | copy-start | bytes 3076
  481.5 161.1 %reduce-scatter.16.cloned.1.call-start = ((), (), s32[]{:S(2)}) async-start(), calls=%async_computation.23 | async-start | bytes 655360 | tf_op jit(solution)/shard_map/reduce_scatter | solution.py:362
  557.9 101.5 %all-gather.27.cloned.1.call-start = ((), (), s32[]{:S(2)}) async-start(), calls=%async_computation.20 | async-start | bytes 5242880 | tf_op jit(solution)/shard_map/all_gather | solution.py:194
  561.3 131.6 %reduce-scatter.14.cloned.1.call-start = ((), (), s32[]{:S(2)}) async-start(), calls=%async_computation.22 | async-start | bytes 1310720 | tf_op jit(solution)/shard_map/reduce_scatter | solution.py:368
  642.5 79.0 %all-gather.29.cloned.1.call-start = ((), (), s32[]{:S(2)}) async-start(), calls=%async_computation.24 | async-start | bytes 1179648 | tf_op jit(solution)/shard_map/all_gather | solution.py:194
  643.1 156.8 %reduce-scatter.8.cloned.1.call-start = ((), (), s32[]{:S(2)}) async-start(), calls=%async_computation.16 | async-start | bytes 4718592 | tf_op jit(solution)/shard_map/reduce_scatter | solution.py:202
  654.8 32.5 %all-to-all-start.2 = ((bf16[8,256,256]{1,2,0:T(8,128)(2,1)}), bf16[8,256,256]{1,2,0:T(8,128)(2,1)}, u32[]{:S(2)}, u32[]{:S(2)}) async-start(bf16[8,256,256]{1,2,0:T(8,128)(2,1)} %copy.99), calls=%async_computation.4 | async-start | bytes 2097152 | tf_op jit(solution)/shard_map/all_to_all | solution.py:198
  659.1 162.3 %reduce-scatter.12.cloned.1.call-start = ((), (), s32[]{:S(2)}) async-start(), calls=%async_computation.21 | async-start | bytes 122880 | tf_op jit(solution)/shard_map/reduce_scatter | solution.py:389
  692.8 179.8 %all-gather.31.cloned.1.call-start = ((), (), s32[]{:S(2)}) async-start(), calls=%async_computation.27 | async-start | bytes 2359296 | tf_op jit(solution)/shard_map/all_gather | solution.py:371
  693.4 225.1 %reduce-scatter.20.cloned.1.call-start = ((), (), s32[]{:S(2)}) async-start(), calls=%async_computation.26 | async-start | bytes 5242880 | tf_op jit(solution)/shard_map/reduce_scatter | solution.py:329
  703.4 289.6 %reduce-scatter.18.cloned.1.call-start = ((), (), s32[]{:S(2)}) async-start(), calls=%async_computation.25 | async-start | bytes 10485760 | tf_op jit(solution)/shard_map/reduce_scatter | solution.py:328
  720.9 79.0 %copy-start.5 = (bf16[256,1024]{1,0:T(8,128)(2,1)S(1)}, bf16[256,1024]{1,0:T(8,128)(2,1)}, u32[]{:S(2)}) copy-start(bf16[256,1024]{1,0:T(8,128)(2,1)} %param.13) | copy-start | bytes 1572868
  720.9 79.0 %copy-start.18 = (f32[256]{0:T(256)S(1)}, f32[256]{0:T(256)}, u32[]{:S(2)}) copy-start(f32[256]{0:T(256)} %copy-done.17) | copy-start | bytes 3076
  721.5 139.5 %all-to-all-start.3 = ((f32[4,256,256]{2,1,0:T(8,128)}), f32[4,256,256]{2,1,0:T(8,128)}, u32[]{:S(2)}, u32[]{:S(2)}) async-start(f32[4,256,256]{2,1,0:T(8,128)} %bitcast.173), calls=%async_computation.8 | async-start | bytes 2097152 | tf_op jit(solution)/shard_map/all_to_all | solution.py:365
  (34 other events, 637.1 us)
Sparse Core Ops, SparseCore 0:
  19.0 74.5 all-gather.12
  95.2 21.0 all-gather.14
  153.6 72.1 all-gather.16
  227.2 32.9 all-gather.18
  261.6 22.8 all-gather.20
  286.4 72.7 all-gather.22
  389.6 86.8 reduce-scatter.9
  481.6 72.4 all-gather.24
  558.0 20.1 reduce-scatter.15
  579.6 34.5 all-gather.26
  642.6 23.3 reduce-scatter.13
  668.0 41.0 all-gather.28
  712.7 87.0 reduce-scatter.7
  802.1 19.2 reduce-scatter.11
  823.4 49.2 all-gather.30
  875.6 42.9 reduce-scatter.19
  921.6 71.3 reduce-scatter.17
